TPU v7x, 128 devices: a whole 4x4x4 slice. The times are simulated.
128 devices in a mesh: wide: 16 (over x, y_hi, core), narrow: 8 (over z, y_lo).
Axes of the slice: x: 4, y: 4 (y_hi: 2, y_lo: 2; y = y_hi * 2 + y_lo), z: 4, core: 2. Of those that a mesh axis runs over, the one named last changes fastest.
Arguments:
- dosages: int32 [2048, 24576], P('narrow', 'wide'), may hold values from 0 to 3, as said below
- allele_counts: int32 [2048], P('narrow'), may hold values from 4000 to 384000, as said below
- called_counts: int32 [2048], P('narrow'), may hold values from 200000 to 400000
Outputs:
- relation: float32 [16, 8, 192, 24576], P(None, 'narrow', None, 'wide')
Inputs may be any that keep to these rules, and one draw needn't show every extreme that they name: 3 marks a missing call; 0, 1 and 2 are dosages. `allele_counts`: the floor of the SNP's called_counts times a whole number p from 1 to 48, divided by 50, so that freq lies in (0, 0.5).
All inputs are finite; a program needn't handle non-finite values.
Results may differ from a plain program's by a relative error of at most 0.0043.
Values may be sent and summed in bfloat16 or wider, within the bound.
A program may use at most 128 MiB of HBM per device.

v0:
```python
import jax
import jax.numpy as jnp
from jax import lax
from jax.sharding import PartitionSpec as P

SNPS = 2048


def standardize(dosages, allele_counts, called_counts):
    freq = allele_counts.astype(jnp.float32) / (2.0 * called_counts.astype(jnp.float32))
    freq = freq[:, None]
    values = (dosages.astype(jnp.float32) - 2.0 * freq) * lax.rsqrt(2.0 * freq * (1.0 - freq))
    values = jnp.where(dosages == 3, jnp.zeros_like(values), values)
    return values.astype(jnp.bfloat16)


def shards(dosages, allele_counts, called_counts):
    standard = standardize(dosages, allele_counts, called_counts)
    sub_width = standard.shape[1] // lax.axis_size("narrow")
    block_rows = lax.all_gather(standard, "narrow", axis=0, tiled=True)
    position = lax.axis_index("narrow") * sub_width
    panel = lax.dynamic_slice_in_dim(block_rows, position, sub_width, 1)
    col_count = block_rows.shape[1]
    gathered = lax.all_gather(panel, "wide", axis=1, tiled=True)
    result = (
        lax.dot_general(
            gathered, block_rows, (((0,), (0,)), ((), ())), preferred_element_type=jnp.float32
        )
        / SNPS
    )
    return result.reshape(lax.axis_size("wide"), 1, sub_width, col_count)


def solution(mesh):
    return jax.shard_map(
        shards,
        mesh=mesh,
        in_specs=(P("narrow", "wide"), P("narrow"), P("narrow")),
        out_specs=P(None, "narrow", None, "wide"),
        check_vma=False,
    )
```

profile of v0, /device:TPU:1, one launch (start us, length us, event | category | flops | bytes accessed | tf_op | source)
XLA Modules:
  0.0 269.7 jit_solution(2306122670743038809)
XLA Ops:
  6.5 0.0 all-gather.3.cloned.1.call-start
  6.5 0.7 broadcast_multiply_fusion
  7.2 1.9 copy.5
  9.1 1.2 select_convert_fusion
  10.3 0.0 all-gather.3.cloned.1.call-update
  10.3 0.0 all-gather.5.cloned.1.call-start
  10.4 131.8 %all-gather.3.cloned.1.call-done = bf16[2048,1536]{0,1:T(8,128)(2,1)} async-done(((bf16[256,1536]{0,1:T(8,128)(2,1)}), bf16[2048,1536]{0,1:T(8,128)(2,1)}) %all-gather.3.cloned.1.call-update) | async-done | bytes 6291472 | tf_op jit(solution)/shard_map/all_gather | solution.py:20
  142.2 2.1 constant_dynamic-slice_fusion
  144.3 0.0 all-gather.5.cloned.1.call-update
  144.4 92.3 %all-gather.5.cloned.1.call-done = bf16[2048,3072]{0,1:T(8,128)(2,1)} async-done(((bf16[2048,192]{0,1:T(8,128)(2,1)}), bf16[2048,3072]{0,1:T(8,128)(2,1)}) %all-gather.5.cloned.1.call-update) | async-done | bytes 12582928 | tf_op jit(solution)/shard_map/all_gather | solution.py:24
  236.6 26.2 %convolution_multiply_fusion = f32[3072,1536]{1,0:T(8,128)} fusion(bf16[2048,3072]{0,1:T(8,128)(2,1)} %all-gather.5.cloned.1.call-done, bf16[2048,1536]{0,1:T(8,128)(2,1)} %all-gather.3.cloned.1.call-done), kind=kOutput, calls=%fused_computation | convolution fusion | flops 19332071424 | bytes 37748736 | tf_op jit(solution)/shard_map/dot_general | solution.py:26
  (1 shorter events, 0.0 us)
Async XLA Ops:
  6.5 135.7 %all-gather.3.cloned.1.call-start = ((), (), s32[]{:S(2)}) async-start(), calls=%async_computation | async-start | bytes 7077888 | tf_op jit(solution)/shard_map/all_gather | solution.py:20
  10.3 226.3 %all-gather.5.cloned.1.call-start = ((), (), s32[]{:S(2)}) async-start(), calls=%async_computation.1 | async-start | bytes 13369344 | tf_op jit(solution)/shard_map/all_gather | solution.py:24
Sparse Core Ops, SparseCore 0:
  10.5 131.7 all-gather.2
  144.6 91.9 all-gather.4
where the time goes:
time: 270 us
  waiting for transfers between devices  224 us (83%)
  matrix products  26.2 us (10%)
  between operations  13.4 us (5%)
  local copies, waits for them, and re-layouts  3.97 us (1%)
    all_gather x1, waiting for transfers between devices, shards(): block_rows = lax.all_gather(standard, 'narrow', axis=0, tiled=True)  132 us
    all_gather x1, waiting for transfers between devices, shards(): gathered = lax.all_gather(panel, 'wide', axis=1, tiled=True)  92.3 us
    dot_general x1, matrix products, shards(): lax.dot_general(gathered, block_rows, (((0,), (0,)), ((), ())), preferred...  26.2 us
  transfers between devices with their start and end apart: 2, of which 2 were waited for; matrix products, arithmetic and copies ran while one was open for 0% of the time, Pallas kernels for 0%

commit v1 on v0

--- a/solution.py
+++ b/solution.py
@@ -21,7 +21,10 @@
     position = lax.axis_index("narrow") * sub_width
     panel = lax.dynamic_slice_in_dim(block_rows, position, sub_width, 1)
     col_count = block_rows.shape[1]
-    gathered = lax.all_gather(panel, "wide", axis=1, tiled=True)
+    long_array = tuple((panel for _ in range(jax.lax.axis_size("wide"))))
+    item_now = jnp.stack(long_array, axis=0)
+    spare = jax.lax.all_to_all(item_now, "wide", 0, 0)
+    gathered = jnp.concatenate(spare, 1)
     result = (
         lax.dot_general(
             gathered, block_rows, (((0,), (0,)), ((), ())), preferred_element_type=jnp.float32

time: 270 us -> 332 us (1.23)
  blocking collectives: 0 us -> 148 us
  waiting for transfers between devices: 224 us -> 132 us
  local copies, waits for them, and re-layouts: 3.97 us -> 8.73 us
    all_to_all x0 -> x1, blocking collectives: none -> 148 us  [shards(): spare = jax.lax.all_to_all(item_now, 'wide', 0, 0)]
    all_gather x1 -> x0, waiting for transfers between devices: 92.3 us -> none  [shards(): gathered = lax.all_gather(panel, 'wide', axis=1, tiled=True)]
    another operation x0 -> x1, local copies, waits for them, and re-layouts: none -> 6.38 us  [shards(): item_now = jnp.stack(long_array, axis=0)]
  transfers between devices with their start and end apart: 2 -> 1, of which waited for: 2 -> 1; matrix products, arithmetic and copies ran while one was open for 0% -> 0% of each run, Pallas kernels for 0% -> 0%
where the time goes in v1:
time: 332 us; the launch traced here: 331 us
  blocking collectives  148 us (45%)
  waiting for transfers between devices  132 us (40%)
  matrix products  24.9 us (8%)
  between operations  13.4 us (4%)
  local copies, waits for them, and re-layouts  8.73 us (3%)
  other arithmetic  3.91 us (1%)
    all_to_all x1, blocking collectives, shards(): spare = jax.lax.all_to_all(item_now, 'wide', 0, 0)  148 us
    all_gather x1, waiting for transfers between devices, shards(): block_rows = lax.all_gather(standard, 'narrow', axis=0, tiled=True)  132 us
    dot_general x1, matrix products, shards(): lax.dot_general(gathered, block_rows, (((0,), (0,)), ((), ())), preferred...  24.9 us
  transfers between devices with their start and end apart: 1, of which 1 were waited for; matrix products, arithmetic and copies ran while one was open for 0% of the time, Pallas kernels for 0%

profile of v1, /device:TPU:1, one launch (start us, length us, event | category | flops | bytes accessed | tf_op | source)
XLA Modules:
  0.0 331.4 jit_solution(14727873375693200377)
XLA Ops:
  6.5 0.0 all-gather.2.cloned.1.call-start
  6.5 0.7 broadcast_multiply_fusion
  7.2 3.2 select_convert_fusion
  10.5 0.0 all-gather.2.cloned.1.call-update
  10.5 132.5 %all-gather.2.cloned.1.call-done = bf16[2048,1536]{1,0:T(8,128)(2,1)} async-done(((bf16[256,1536]{1,0:T(8,128)(2,1)}), bf16[2048,1536]{1,0:T(8,128)(2,1)}) %all-gather.2.cloned.1.call-update) | async-done | bytes 6291472 | tf_op jit(solution)/shard_map/all_gather | solution.py:20
  143.0 1.8 constant_dynamic-slice_fusion
  144.8 0.5 copy.5
  145.3 6.4 %stack.2 = bf16[16,2048,192]{1,2,0:T(8,128)(2,1)} broadcast(bf16[2048,192]{0,1:T(8,128)(2,1)S(1)} %copy.5), dimensions={1,2} | broadcast | bytes 13369344 | tf_op jit(solution)/shard_map/stack | solution.py:25
  151.7 148.0 %all_to_all.5 = bf16[16,2048,192]{1,2,0:T(8,128)(2,1)S(1)} all-to-all(bf16[16,2048,192]{1,2,0:T(8,128)(2,1)} %stack.2), channel_id=1, replica_groups=mesh['wide'=16,'narrow'=8] {'wide'}, dimensions={0} | all-to-all | bytes 25165824 | tf_op jit(solution)/shard_map/all_to_all | solution.py:26
  299.7 24.9 %convolution_multiply_fusion = f32[3072,1536]{1,0:T(8,128)} fusion(bf16[2048,3072]{0,1:T(8,128)(2,1)S(1)} %bitcast.8, bf16[2048,1536]{1,0:T(8,128)(2,1)} %all-gather.2.cloned.1.call-done), kind=kOutput, calls=%fused_computation | convolution fusion | flops 19332071424 | bytes 37748736 | tf_op jit(solution)/shard_map/dot_general | solution.py:29
  (1 shorter events, 0.0 us)
Async XLA Ops:
  6.5 136.4 %all-gather.2.cloned.1.call-start = ((), (), s32[]{:S(2)}) async-start(), calls=%async_computation.1 | async-start | bytes 7077888 | tf_op jit(solution)/shard_map/all_gather | solution.py:20
Sparse Core Ops, SparseCore 0:
  10.6 132.3 all-gather.1
